TPU v7x, 512 devices: a whole 4x8x8 slice. The times are simulated.
512 devices in a mesh: freq: 16 (over y, core), offset: 32 (over x, z).
Axes of the slice: x: 4, y: 8, z: 8, core: 2. Of those that a mesh axis runs over, the one named last changes fastest.
Arguments:
- raw_traces: bfloat16 [32768, 2048], P('offset', 'freq'), may hold values from -6 to 6
- trace_slot: int32 [32, 1024], P(None, 'offset'), may hold values from 0 to 1023, as said below
- offset_index: int32 [1024], replicated, may hold values from 1 to 1023
- slowness_index: int32 [256], replicated, may hold values from 0 to 511
Outputs:
- radon: float32 [256, 1024, 64], P('offset', 'freq')
Inputs may be any that keep to these rules, and one draw needn't show every extreme that they name: `trace_slot`: in every aligned block of 32 columns, the 32 x 32 entries name each of 0 to 1023 exactly once.
All inputs are finite; a program needn't handle non-finite values.
Results may differ from a plain program's by a relative error of at most 0.0046.
Values may be sent and summed in bfloat16 or wider, within the bound.
A program may use at most 64 MiB of HBM per device.

v0:
```python
import math
import jax
import jax.numpy as jnp
from jax import lax
from jax.sharding import Mesh
from jax.sharding import PartitionSpec as P

NF = 1024
OFFSET = ("offset_0", "offset_1")
APEX_TIME = 100.0
CURVATURE = 0.0003


def own_rows(total, axes):
    for axis in axes:
        total = lax.psum_scatter(total, axis, scatter_dimension=0, tiled=True)
    return total


def moveout(slowness, offset_grid):
    spread = (
        CURVATURE * slowness.astype(jnp.float32)[:, None] * offset_grid.astype(jnp.float32)[None, :]
    )
    return jnp.sqrt(APEX_TIME * APEX_TIME + spread * spread) - APEX_TIME


def whole_table(local_freqs, total_time):
    column_total = 2 * NF
    column = jnp.arange(column_total, dtype=jnp.int32)
    band_ids = column // (2 * local_freqs)
    within = column % (2 * local_freqs)
    freq_ids = band_ids * local_freqs + within % local_freqs
    shifts = jnp.where(within < local_freqs, 0, total_time // 2).astype(jnp.int32)
    odd_rates = 2 * freq_ids + 1
    fine_size = 64
    coarse_size = total_time // fine_size
    period = 2 * total_time
    coarse_ids = jnp.arange(coarse_size, dtype=jnp.int32)[:, None]
    fine_ids = jnp.arange(fine_size, dtype=jnp.int32)[:, None]
    coarse_turn = coarse_ids * fine_size % period * odd_rates[None, :] % period
    fine_turn = (fine_ids * odd_rates[None, :] + shifts[None, :]) % period
    coarse_angle = coarse_turn.astype(jnp.float32) * (math.pi / total_time)
    fine_angle = fine_turn.astype(jnp.float32) * (math.pi / total_time)
    coarse_cos = jnp.cos(coarse_angle)
    coarse_sin = jnp.sin(coarse_angle)
    fine_cos = jnp.cos(fine_angle)
    fine_sin = jnp.sin(fine_angle)
    values = (
        coarse_cos[:, None, :] * fine_cos[None, :, :]
        - coarse_sin[:, None, :] * fine_sin[None, :, :]
    )
    values = values.reshape(total_time, column_total)
    return (values * (1.0 / math.sqrt(total_time))).astype(jnp.bfloat16)


def local(raw_traces, trace_slot, offset_index, slowness_index):
    gathers, local_offsets = trace_slot.shape
    local_times = raw_traces.shape[1]
    freq_devices = lax.axis_size("freq")
    offset_devices = lax.axis_size(OFFSET)
    total_time = local_times * freq_devices
    local_freqs = NF // freq_devices
    trace_rows = gathers * local_offsets
    picked = raw_traces[trace_slot.reshape(-1)]
    grouped = picked.reshape(freq_devices, trace_rows // freq_devices, local_times)
    fourier_table = whole_table(local_freqs, total_time)
    series = lax.all_to_all(grouped, "freq", split_axis=0, concat_axis=2, tiled=True)
    flattened = series.reshape(series.shape[1], total_time)
    spectrum = jnp.dot(flattened, fourier_table, preferred_element_type=jnp.float32).astype(
        jnp.bfloat16
    )
    spectrum = jnp.transpose(
        spectrum.reshape(flattened.shape[0], freq_devices, 2 * local_freqs), (1, 0, 2)
    )
    assembled = lax.all_to_all(spectrum, "freq", split_axis=0, concat_axis=0, tiled=True)
    spectra = assembled.reshape(gathers, local_offsets, 2 * local_freqs)
    real_part = spectra[:, :, :local_freqs]
    imag_part = spectra[:, :, local_freqs:]
    freq_ids = lax.axis_index("freq") * local_freqs + jnp.arange(local_freqs, dtype=jnp.int32)
    angular = (2 * freq_ids + 1).astype(jnp.float32) * (math.pi / total_time)
    own_offsets = lax.dynamic_slice_in_dim(
        offset_index, lax.axis_index(OFFSET) * local_offsets, local_offsets
    )
    delays = moveout(slowness_index, own_offsets)
    phases = angular[:, None, None] * delays[None, :, :]
    cosine = jnp.cos(phases).astype(jnp.bfloat16)
    sines = jnp.sin(phases).astype(jnp.bfloat16)
    real_out = jnp.einsum(
        "fph,ghf->pfg", cosine, real_part, preferred_element_type=jnp.float32
    ) - jnp.einsum("fph,ghf->pfg", sines, imag_part, preferred_element_type=jnp.float32)
    imag_out = jnp.einsum(
        "fph,ghf->pfg", sines, real_part, preferred_element_type=jnp.float32
    ) + jnp.einsum("fph,ghf->pfg", cosine, imag_part, preferred_element_type=jnp.float32)
    summed = own_rows(jnp.concatenate([real_out, imag_out], axis=2), OFFSET)
    return summed * (1.0 / math.sqrt(local_offsets * offset_devices))


def solution(mesh):
    torus = Mesh(mesh.devices.reshape(mesh.shape["freq"], 4, 8), ("freq", "offset_0", "offset_1"))
    placed = (P(OFFSET, "freq"), P(None, OFFSET), P(), P())
    return jax.shard_map(
        local, mesh=torus, in_specs=placed, out_specs=P(OFFSET, "freq", None), check_vma=False
    )
```

profile of v0, /device:TPU:8, one launch (start us, length us, event | category | flops | bytes accessed | tf_op | source)
XLA Modules:
  0.0 206.7 jit_solution(16207781302193923566)
XLA Ops:
  6.5 0.0 copy-start
  6.5 0.8 reshape.308
  7.4 0.1 copy-done
  7.5 4.3 %gather_fusion = bf16[1024,128]{1,0:T(8,128)(2,1)} fusion(bf16[1024,128]{1,0:T(8,128)(2,1)S(1)} %copy-done, s32[1024]{0:T(1024)S(1)} %broadcast_clamp_fusion), kind=kCustom, calls=%fused_computation | custom fusion | bytes 528384 | tf_op jit(solution)/shard_map/gather | solution.py:64
  11.8 9.1 %all-to-all-start = ((bf16[16,64,128]{2,1,0:T(8,128)(2,1)}), bf16[16,64,128]{2,1,0:T(8,128)(2,1)S(1)}, u32[]{:S(2)}, u32[]{:S(2)}) async-start(bf16[16,64,128]{2,1,0:T(8,128)(2,1)} %bitcast.1), calls=%async_computation | async-start | bytes 524288 | tf_op jit(solution)/shard_map/all_to_all | solution.py:67
  21.0 2.1 fusion.21
  23.0 1.1 fusion.28
  24.1 6.2 %multiply_convert_fusion = bf16[32,64,2048]{2,1,0:T(8,128)(2,1)} fusion(f32[64,2048]{1,0:T(8,128)S(1)} %get-tuple-element.8, f32[32,2048]{1,0:T(8,128)S(1)} %get-tuple-element.10, f32[64,2048]{1,0:T(8,128)S(1)} %get-tuple-element.7, f32[32,2048]{1,0:T(8,128)S(1)} %get-tuple-element.9), kind=kLoop, calls=%fused_computation.1 | loop fusion | flops 20971520 | bytes 9961472 | tf_op jit(solution)/shard_map/convert_element_type | solution.py:53
  30.3 0.3 all-to-all-done
  30.6 0.2 copy.12
  30.8 0.0 copy-start.1
  30.8 5.0 %fusion.8 = bf16[8,16,8,128]{3,2,1,0:T(8,128)(2,1)S(1)} fusion(bf16[2048,2048]{1,0:T(8,128)(2,1)} %bitcast.32, bf16[8,8,16,128]{3,2,1,0:T(8,128)(2,1)S(1)} %bitcast.36), kind=kOutput, calls=%fused_computation.12 | convolution fusion | flops 537001984 | bytes 8912896 | tf_op jit(solution)/shard_map/dot_general | solution.py:69
  35.7 0.8 copy.30
  36.5 7.0 %all-to-all-start.1 = ((bf16[16,64,128]{2,1,0:T(8,128)(2,1)}), bf16[16,64,128]{2,1,0:T(8,128)(2,1)S(1)}, u32[]{:S(2)}, u32[]{:S(2)}) async-start(bf16[16,64,128]{2,1,0:T(8,128)(2,1)} %bitcast.31), calls=%async_computation.1 | async-start | bytes 524288 | tf_op jit(solution)/shard_map/all_to_all | solution.py:75
  43.5 0.2 reduce-scatter.7.cloned.1.call-start
  43.7 0.8 dynamic-slice_convert_fusion
  44.5 0.0 copy-done.1
  44.5 0.1 sqrt_add_fusion
  44.6 8.5 %all-to-all-done.1 = bf16[16,64,128]{2,1,0:T(8,128)(2,1)S(1)} async-done(((bf16[16,64,128]{2,1,0:T(8,128)(2,1)}), bf16[16,64,128]{2,1,0:T(8,128)(2,1)S(1)}, u32[]{:S(2)}, u32[]{:S(2)}) %all-to-all-start.1) | async-done | bytes 262176 | tf_op jit(solution)/shard_map/all_to_all | solution.py:75
  53.1 0.1 fusion.44
  53.3 0.8 copy.21
  54.0 8.5 %fusion.2 = f32[64,32,256]{2,1,0:T(8,128)} fusion(bf16[32,32,64]{1,0,2:T(8,128)(2,1)S(1)} %copy.21, f32[256,32]{0,1:T(8,128)S(1)} %sqrt_add_fusion, f32[64]{0:T(128)S(1)} %convert_multiply_fusion.1), kind=kOutput, calls=%fused_computation.10 | convolution fusion | flops 34603008 | bytes 2261248 | tf_op jit(solution)/shard_map/fph,ghf->pfg/dot_general | solution.py:91
  62.5 6.9 %fusion.6 = f32[64,32,256]{2,1,0:T(8,128)S(1)} fusion(bf16[32,32,64]{1,0,2:T(8,128)(2,1)S(1)} %copy.21, f32[256,32]{0,1:T(8,128)S(1)} %sqrt_add_fusion, f32[64]{0:T(128)S(1)} %convert_multiply_fusion.1), kind=kOutput, calls=%fused_computation.11 | convolution fusion | flops 34603008 | bytes 2261248 | tf_op jit(solution)/shard_map/fph,ghf->pfg/dot_general | solution.py:88
  69.4 0.8 copy.22
  70.2 9.6 %add_bitcast_fusion = f32[256,64,32]{0,2,1:T(8,128)S(1)} fusion(f32[64,32,256]{2,1,0:T(8,128)} %fusion.2, bf16[32,32,64]{1,0,2:T(8,128)(2,1)S(1)} %copy.22, f32[256,32]{0,1:T(8,128)S(1)} %sqrt_add_fusion, f32[64]{0:T(128)S(1)} %convert_multiply_fusion.1), kind=kOutput, calls=%fused_computation.8 | convolution fusion | flops 35127296 | bytes 4358400 | tf_op jit(solution)/shard_map/fph,ghf->pfg/dot_general | solution.py:93
  79.8 7.0 %subtract_bitcast_fusion = f32[256,64,32]{0,2,1:T(8,128)S(1)} fusion(f32[64,32,256]{2,1,0:T(8,128)S(1)} %fusion.6, bf16[32,32,64]{1,0,2:T(8,128)(2,1)S(1)} %copy.22, f32[256,32]{0,1:T(8,128)S(1)} %sqrt_add_fusion, f32[64]{0:T(128)S(1)} %convert_multiply_fusion.1), kind=kOutput, calls=%fused_computation.9 | convolution fusion | flops 35127296 | bytes 4358400 | tf_op jit(solution)/shard_map/fph,ghf->pfg/dot_general | solution.py:90
  86.8 2.2 %pad_maximum_fusion = f32[256,64,64]{0,2,1:T(8,128)} fusion(f32[256,64,32]{0,2,1:T(8,128)S(1)} %add_bitcast_fusion, f32[256,64,32]{0,2,1:T(8,128)S(1)} %subtract_bitcast_fusion), kind=kLoop, calls=%fused_computation.2 | loop fusion | flops 1048576 | bytes 8388608 | tf_op jit(solution)/shard_map/concatenate | solution.py:94
  89.0 5.6 %copy.19 = f32[256,4096]{1,0:T(8,128)} copy(f32[256,4096]{0,1:T(8,128)} %bitcast.33) | data formatting | bytes 8388608
  94.7 0.0 reduce-scatter.7.cloned.1.call-update
  94.7 0.0 reduce-scatter.5.cloned.1.call-start
  94.7 52.6 %reduce-scatter.7.cloned.1.call-done = f32[64,4096]{1,0:T(8,128)} async-done(((f32[256,4096]{1,0:T(8,128)}), f32[64,4096]{1,0:T(8,128)}) %reduce-scatter.7.cloned.1.call-update) | async-done | bytes 1048592
  147.4 1.8 copy.20
  149.2 2.7 %copy.16 = f32[64,64,64]{2,1,0:T(8,128)} copy(f32[64,64,64]{0,2,1:T(8,128)S(1)} %bitcast.34) | data formatting | bytes 2097152 | tf_op jit(solution)/shard_map/reduce_scatter | solution.py:16
  151.9 0.0 reduce-scatter.5.cloned.1.call-update
  151.9 46.2 %reduce-scatter.5.cloned.1.call-done = f32[8,64,64]{2,1,0:T(8,128)} async-done(((f32[64,64,64]{2,1,0:T(8,128)}), f32[8,64,64]{2,1,0:T(8,128)}) %reduce-scatter.5.cloned.1.call-update) | async-done | bytes 131088 | tf_op jit(solution)/shard_map/reduce_scatter | solution.py:16
  198.1 1.7 broadcast_multiply_fusion
  (6 shorter events, 0.0 us)
Async XLA Ops:
  6.5 1.0 copy-start
  11.8 18.8 %all-to-all-start = ((bf16[16,64,128]{2,1,0:T(8,128)(2,1)}), bf16[16,64,128]{2,1,0:T(8,128)(2,1)S(1)}, u32[]{:S(2)}, u32[]{:S(2)}) async-start(bf16[16,64,128]{2,1,0:T(8,128)(2,1)} %bitcast.1), calls=%async_computation | async-start | bytes 524288 | tf_op jit(solution)/shard_map/all_to_all | solution.py:67
  30.8 13.7 %copy-start.1 = (s32[256]{0:T(256)S(1)}, s32[256]{0:T(256)}, u32[]{:S(2)}) copy-start(s32[256]{0:T(256)} %param.7) | copy-start | bytes 3076
  36.5 16.6 %all-to-all-start.1 = ((bf16[16,64,128]{2,1,0:T(8,128)(2,1)}), bf16[16,64,128]{2,1,0:T(8,128)(2,1)S(1)}, u32[]{:S(2)}, u32[]{:S(2)}) async-start(bf16[16,64,128]{2,1,0:T(8,128)(2,1)} %bitcast.31), calls=%async_computation.1 | async-start | bytes 524288 | tf_op jit(solution)/shard_map/all_to_all | solution.py:75
  43.5 103.9 %reduce-scatter.7.cloned.1.call-start = ((), (), s32[]{:S(2)}) async-start(), calls=%async_computation.5 | async-start | bytes 5242880
  94.7 103.5 %reduce-scatter.5.cloned.1.call-start = ((), (), s32[]{:S(2)}) async-start(), calls=%async_computation.4 | async-start | bytes 2359296 | tf_op jit(solution)/shard_map/reduce_scatter | solution.py:16
Sparse Core Ops, SparseCore 0:
  94.8 52.5 reduce-scatter.6
  152.1 46.0 reduce-scatter.4
where the time goes:
time: 207 us
  waiting for transfers between devices  108 us (52%)
  matrix products  36.9 us (18%)
  local copies, waits for them, and re-layouts  18.1 us (9%)
  starting transfers between devices  16.4 us (8%)
  other arithmetic  14.1 us (7%)
  between operations  13.5 us (7%)
    unnamed x3, waiting for transfers between devices  52.7 us
    reduce_scatter x1, waiting for transfers between devices, own_rows(): total = lax.psum_scatter(total, axis, scatter_dimension=0, tiled=True)  46.2 us
    dot_general x1, matrix products, local(): jnp.einsum('fph,ghf->pfg', cosine, imag_part, preferred_element_type=jnp....  9.6 us
    all_to_all x1, starting transfers between devices, local(): lax.all_to_all(grouped, 'freq', split_axis=0, concat_axis=2, tiled=True)  9.12 us
    unnamed x8, local copies, waits for them, and re-layouts  9.12 us
    all_to_all x1, waiting for transfers between devices, local(): lax.all_to_all(spectrum, 'freq', split_axis=0, concat_axis=0, tiled=True)  8.5 us
    dot_general x1, matrix products, local(): jnp.einsum('fph,ghf->pfg', sines, real_part, preferred_element_type=jnp.f...  8.45 us
    dot_general x1, matrix products, local(): jnp.einsum('fph,ghf->pfg', sines, imag_part, preferred_element_type=jnp.f...  7.03 us
  transfers between devices with their start and end apart: 4, of which 4 were waited for; matrix products, arithmetic and copies ran while one was open for 5% of the time, Pallas kernels for 0%

commit v1 on v0

--- a/solution.py
+++ b/solution.py
@@ -9,6 +9,18 @@
 OFFSET = ("offset_0", "offset_1")
 APEX_TIME = 100.0
 CURVATURE = 0.0003
+
+
+def split_up(x, dim, size):
+    shape = x.shape
+    blocks = x.reshape(*shape[:dim], size, shape[dim] // size, *shape[dim + 1 :])
+    return jnp.moveaxis(blocks, dim, 0)
+
+
+def joined_along(tiles, dim):
+    tiles = jnp.moveaxis(tiles, 0, dim)
+    shape = tiles.shape
+    return tiles.reshape(*shape[:dim], shape[dim] * shape[dim + 1], *shape[dim + 2 :])
 
 
 def own_rows(total, axes):
@@ -72,7 +84,14 @@
     spectrum = jnp.transpose(
         spectrum.reshape(flattened.shape[0], freq_devices, 2 * local_freqs), (1, 0, 2)
     )
-    assembled = lax.all_to_all(spectrum, "freq", split_axis=0, concat_axis=0, tiled=True)
+    peers, index = (lax.axis_size("freq"), lax.axis_index("freq"))
+    pieces = split_up(spectrum, 0, peers)
+    outs = [pieces[index]]
+    for lap in range(1, peers):
+        sent = pieces[index ^ lap]
+        outs.append(lax.ppermute(sent, "freq", [(i, i ^ lap) for i in range(peers)]))
+    pieces = jnp.stack(outs)[index ^ jnp.arange(peers)]
+    assembled = joined_along(pieces, 0)
     spectra = assembled.reshape(gathers, local_offsets, 2 * local_freqs)
     real_part = spectra[:, :, :local_freqs]
     imag_part = spectra[:, :, local_freqs:]

time: 207 us -> 253 us (1.22)
  the two profiles are of different devices: /device:TPU:8 before, /device:TPU:2 now
where the time goes in v1:
time: 253 us; the launch traced here: 252 us
  waiting for transfers between devices  106 us (42%)
  starting transfers between devices  61.7 us (24%)
  matrix products  36.9 us (15%)
  local copies, waits for them, and re-layouts  19 us (8%)
  other arithmetic  14.2 us (6%)
  between operations  14 us (6%)
    unnamed x3, waiting for transfers between devices  54.8 us
    ppermute x15, starting transfers between devices, local(): lax.ppermute(sent, 'freq', [(i, i ^ lap) for i in range(peers)])  54.4 us
    reduce_scatter x1, waiting for transfers between devices, own_rows(): total = lax.psum_scatter(total, axis, scatter_dimension=0, tiled=True)  47.5 us
    dot_general x1, matrix products, local(): jnp.einsum('fph,ghf->pfg', cosine, imag_part, preferred_element_type=jnp....  9.6 us
    unnamed x39, local copies, waits for them, and re-layouts  9.41 us
    dot_general x1, matrix products, local(): jnp.einsum('fph,ghf->pfg', sines, real_part, preferred_element_type=jnp.f...  8.46 us
    all_to_all x1, starting transfers between devices, local(): lax.all_to_all(grouped, 'freq', split_axis=0, concat_axis=2, tiled=True)  7.21 us
    dot_general x1, matrix products, local(): jnp.einsum('fph,ghf->pfg', sines, imag_part, preferred_element_type=jnp.f...  7.03 us
  transfers between devices with their start and end apart: 18, of which 5 were waited for; matrix products, arithmetic and copies ran while one was open for 4% of the time, Pallas kernels for 0%

profile of v1, /device:TPU:2, one launch (start us, length us, event | category | flops | bytes accessed | tf_op | source)
XLA Modules:
  0.0 252.0 jit_solution(1820577896534052213)
XLA Ops:
  6.5 0.0 copy-start
  6.5 0.8 reshape.370
  7.4 0.1 copy-done
  7.5 4.3 %gather_fusion = bf16[1024,128]{1,0:T(8,128)(2,1)} fusion(bf16[1024,128]{1,0:T(8,128)(2,1)S(1)} %copy-done, s32[1024]{0:T(1024)S(1)} %broadcast_clamp_fusion), kind=kCustom, calls=%fused_computation | custom fusion | bytes 528384 | tf_op jit(solution)/shard_map/gather | solution.py:76
  11.8 7.2 %all-to-all-start = ((bf16[16,64,128]{2,1,0:T(8,128)(2,1)}), bf16[16,64,128]{2,1,0:T(8,128)(2,1)S(1)}, u32[]{:S(2)}, u32[]{:S(2)}) async-start(bf16[16,64,128]{2,1,0:T(8,128)(2,1)} %bitcast.1), calls=%async_computation | async-start | bytes 524288 | tf_op jit(solution)/shard_map/all_to_all | solution.py:79
  19.0 0.0 reduce-scatter.7.cloned.1.call-start
  19.1 2.1 fusion.21
  21.2 1.1 fusion.28
  22.3 0.0 copy-start.1
  22.3 6.2 %multiply_convert_fusion = bf16[32,64,2048]{2,1,0:T(8,128)(2,1)} fusion(f32[64,2048]{1,0:T(8,128)S(1)} %get-tuple-element.24, f32[32,2048]{1,0:T(8,128)S(1)} %get-tuple-element.26, f32[64,2048]{1,0:T(8,128)S(1)} %get-tuple-element.23, f32[32,2048]{1,0:T(8,128)S(1)} %get-tuple-element.25), kind=kLoop, calls=%fused_computation.2 | loop fusion | flops 20971520 | bytes 9961472 | tf_op jit(solution)/shard_map/convert_element_type | solution.py:65
  28.5 0.8 dynamic-slice_convert_fusion
  29.3 0.1 sqrt_add_fusion
  29.4 0.8 all-to-all-done
  30.2 0.2 copy.27
  30.3 4.9 %fusion.8 = bf16[8,8,16,128]{3,1,2,0:T(8,128)(2,1)S(1)} fusion(bf16[2048,2048]{1,0:T(8,128)(2,1)} %bitcast.111, bf16[8,8,16,128]{3,2,1,0:T(8,128)(2,1)S(1)} %bitcast.116), kind=kOutput, calls=%fused_computation.13 | convolution fusion | flops 537001984 | bytes 8912896 | tf_op jit(solution)/shard_map/dot_general | solution.py:81
  35.3 0.8 constant_dynamic-slice_fusion
  36.2 2.8 %collective-permute-start = (bf16[1,64,128]{2,1,0:T(8,128)(2,1)S(1)}, bf16[1,64,128]{2,1,0:T(8,128)(2,1)S(1)}, u32[]{:S(2)}, u32[]{:S(2)}) collective-permute-start(bf16[1,64,128]{2,1,0:T(8,128)(2,1)S(1)} %bitcast.133), channel_id=1, source_target_pairs={{0,32},{32,0},{64,96},{96,64},{128,160},{160,128},{192,224},{224,1... | collective-permute-start | bytes 49160 | tf_op jit(solution)/shard_map/ppermute | solution.py:92
  39.0 2.3 collective-permute-start.1
  41.3 2.8 %collective-permute-start.2 = (bf16[1,64,128]{2,1,0:T(8,128)(2,1)S(1)}, bf16[1,64,128]{2,1,0:T(8,128)(2,1)S(1)}, u32[]{:S(2)}, u32[]{:S(2)}) collective-permute-start(bf16[1,64,128]{2,1,0:T(8,128)(2,1)S(1)} %bitcast.131), channel_id=1, source_target_pairs={{0,96},{32,64},{64,32},{96,0},{128,224},{160,192},{192,160},{224,1... | collective-permute-start | bytes 49160 | tf_op jit(solution)/shard_map/ppermute | solution.py:92
  44.2 3.6 %collective-permute-start.3 = (bf16[1,64,128]{2,1,0:T(8,128)(2,1)S(1)}, bf16[1,64,128]{2,1,0:T(8,128)(2,1)S(1)}, u32[]{:S(2)}, u32[]{:S(2)}) collective-permute-start(bf16[1,64,128]{2,1,0:T(8,128)(2,1)S(1)} %bitcast.130), channel_id=1, source_target_pairs={{0,128},{32,160},{64,192},{96,224},{128,0},{160,32},{192,64},{224,... | collective-permute-start | bytes 49160 | tf_op jit(solution)/shard_map/ppermute | solution.py:92
  47.8 3.2 %collective-permute-start.4 = (bf16[1,64,128]{2,1,0:T(8,128)(2,1)S(1)}, bf16[1,64,128]{2,1,0:T(8,128)(2,1)S(1)}, u32[]{:S(2)}, u32[]{:S(2)}) collective-permute-start(bf16[1,64,128]{2,1,0:T(8,128)(2,1)S(1)} %bitcast.129), channel_id=1, source_target_pairs={{0,160},{32,128},{64,224},{96,192},{128,32},{160,0},{192,96},{224,... | collective-permute-start | bytes 49160 | tf_op jit(solution)/shard_map/ppermute | solution.py:92
  51.2 0.0 collective-permute-done
  51.2 4.1 %collective-permute-start.5 = (bf16[1,64,128]{2,1,0:T(8,128)(2,1)S(1)}, bf16[1,64,128]{2,1,0:T(8,128)(2,1)S(1)}, u32[]{:S(2)}, u32[]{:S(2)}) collective-permute-start(bf16[1,64,128]{2,1,0:T(8,128)(2,1)S(1)} %bitcast.128), channel_id=1, source_target_pairs={{0,192},{32,224},{64,128},{96,160},{128,64},{160,96},{192,0},{224,... | collective-permute-start | bytes 49160 | tf_op jit(solution)/shard_map/ppermute | solution.py:92
  55.4 0.0 collective-permute-done.1
  55.4 2.8 %collective-permute-start.6 = (bf16[1,64,128]{2,1,0:T(8,128)(2,1)S(1)}, bf16[1,64,128]{2,1,0:T(8,128)(2,1)S(1)}, u32[]{:S(2)}, u32[]{:S(2)}) collective-permute-start(bf16[1,64,128]{2,1,0:T(8,128)(2,1)S(1)} %bitcast.127), channel_id=1, source_target_pairs={{0,224},{32,192},{64,160},{96,128},{128,96},{160,64},{192,32},{224... | collective-permute-start | bytes 49160 | tf_op jit(solution)/shard_map/ppermute | solution.py:92
  58.2 0.0 collective-permute-done.2
  58.2 6.6 %collective-permute-start.7 = (bf16[1,64,128]{2,1,0:T(8,128)(2,1)S(1)}, bf16[1,64,128]{2,1,0:T(8,128)(2,1)S(1)}, u32[]{:S(2)}, u32[]{:S(2)}) collective-permute-start(bf16[1,64,128]{2,1,0:T(8,128)(2,1)S(1)} %bitcast.126), channel_id=1, source_target_pairs={{0,256},{32,288},{64,320},{96,352},{128,384},{160,416},{192,448},{... | collective-permute-start | bytes 49160 | tf_op jit(solution)/shard_map/ppermute | solution.py:92
  64.9 0.0 collective-permute-done.3
  64.9 3.2 %collective-permute-start.8 = (bf16[1,64,128]{2,1,0:T(8,128)(2,1)S(1)}, bf16[1,64,128]{2,1,0:T(8,128)(2,1)S(1)}, u32[]{:S(2)}, u32[]{:S(2)}) collective-permute-start(bf16[1,64,128]{2,1,0:T(8,128)(2,1)S(1)} %bitcast.125), channel_id=1, source_target_pairs={{0,288},{32,256},{64,352},{96,320},{128,416},{160,384},{192,480},{... | collective-permute-start | bytes 49160 | tf_op jit(solution)/shard_map/ppermute | solution.py:92
  68.2 0.0 collective-permute-done.4
  68.2 3.5 %collective-permute-start.9 = (bf16[1,64,128]{2,1,0:T(8,128)(2,1)S(1)}, bf16[1,64,128]{2,1,0:T(8,128)(2,1)S(1)}, u32[]{:S(2)}, u32[]{:S(2)}) collective-permute-start(bf16[1,64,128]{2,1,0:T(8,128)(2,1)S(1)} %bitcast.124), channel_id=1, source_target_pairs={{0,320},{32,352},{64,256},{96,288},{128,448},{160,480},{192,384},{... | collective-permute-start | bytes 49160 | tf_op jit(solution)/shard_map/ppermute | solution.py:92
  71.7 0.0 collective-permute-done.5
  71.7 4.6 %collective-permute-start.10 = (bf16[1,64,128]{2,1,0:T(8,128)(2,1)S(1)}, bf16[1,64,128]{2,1,0:T(8,128)(2,1)S(1)}, u32[]{:S(2)}, u32[]{:S(2)}) collective-permute-start(bf16[1,64,128]{2,1,0:T(8,128)(2,1)S(1)} %bitcast.123), channel_id=1, source_target_pairs={{0,352},{32,320},{64,288},{96,256},{128,480},{160,448},{192,416},{... | collective-permute-start | bytes 49160 | tf_op jit(solution)/shard_map/ppermute | solution.py:92
  76.4 0.0 collective-permute-done.6
  76.4 3.0 %collective-permute-start.11 = (bf16[1,64,128]{2,1,0:T(8,128)(2,1)S(1)}, bf16[1,64,128]{2,1,0:T(8,128)(2,1)S(1)}, u32[]{:S(2)}, u32[]{:S(2)}) collective-permute-start(bf16[1,64,128]{2,1,0:T(8,128)(2,1)S(1)} %bitcast.122), channel_id=1, source_target_pairs={{0,384},{32,416},{64,448},{96,480},{128,256},{160,288},{192,320},{... | collective-permute-start | bytes 49160 | tf_op jit(solution)/shard_map/ppermute | solution.py:92
  79.5 0.0 collective-permute-done.7
  79.5 5.0 %collective-permute-start.12 = (bf16[1,64,128]{2,1,0:T(8,128)(2,1)S(1)}, bf16[1,64,128]{2,1,0:T(8,128)(2,1)S(1)}, u32[]{:S(2)}, u32[]{:S(2)}) collective-permute-start(bf16[1,64,128]{2,1,0:T(8,128)(2,1)S(1)} %bitcast.121), channel_id=1, source_target_pairs={{0,416},{32,384},{64,480},{96,448},{128,288},{160,256},{192,352},{... | collective-permute-start | bytes 49160 | tf_op jit(solution)/shard_map/ppermute | solution.py:92
  84.5 0.0 collective-permute-done.8
  84.5 3.5 %collective-permute-start.13 = (bf16[1,64,128]{2,1,0:T(8,128)(2,1)S(1)}, bf16[1,64,128]{2,1,0:T(8,128)(2,1)S(1)}, u32[]{:S(2)}, u32[]{:S(2)}) collective-permute-start(bf16[1,64,128]{2,1,0:T(8,128)(2,1)S(1)} %bitcast.120), channel_id=1, source_target_pairs={{0,448},{32,480},{64,384},{96,416},{128,320},{160,352},{192,256},{... | collective-permute-start | bytes 49160 | tf_op jit(solution)/shard_map/ppermute | solution.py:92
  88.1 0.0 collective-permute-done.9
  88.1 3.0 %collective-permute-start.14 = (bf16[1,64,128]{2,1,0:T(8,128)(2,1)S(1)}, bf16[1,64,128]{2,1,0:T(8,128)(2,1)S(1)}, u32[]{:S(2)}, u32[]{:S(2)}) collective-permute-start(bf16[1,64,128]{2,1,0:T(8,128)(2,1)S(1)} %bitcast.119), channel_id=1, source_target_pairs={{0,480},{32,448},{64,416},{96,384},{128,352},{160,320},{192,288},{... | collective-permute-start | bytes 49160 | tf_op jit(solution)/shard_map/ppermute | solution.py:92
  91.2 0.0 collective-permute-done.10
  91.2 0.0 collective-permute-done.11
  91.2 0.0 collective-permute-done.12
  91.2 0.4 collective-permute-done.13
  91.6 2.7 %collective-permute-done.14 = bf16[1,64,128]{2,1,0:T(8,128)(2,1)S(1)} collective-permute-done((bf16[1,64,128]{2,1,0:T(8,128)(2,1)S(1)}, bf16[1,64,128]{2,1,0:T(8,128)(2,1)S(1)}, u32[]{:S(2)}, u32[]{:S(2)}) %collective-permute-start.14) | collective-permute-done | bytes 16416 | tf_op jit(solution)/shard_map/ppermute | solution.py:92
  94.4 0.6 gather_fusion.1
  95.0 0.1 fusion.45
  95.1 0.8 copy.68
  95.9 8.5 %fusion.2 = f32[64,32,256]{2,1,0:T(8,128)} fusion(bf16[32,32,64]{1,0,2:T(8,128)(2,1)S(1)} %copy.68, f32[256,32]{0,1:T(8,128)S(1)} %sqrt_add_fusion, f32[64]{0:T(128)S(1)} %convert_multiply_fusion.1), kind=kOutput, calls=%fused_computation.11 | convolution fusion | flops 34603008 | bytes 2261248 | tf_op jit(solution)/shard_map/fph,ghf->pfg/dot_general | solution.py:110
  104.4 6.9 %fusion.6 = f32[64,32,256]{2,1,0:T(8,128)S(1)} fusion(bf16[32,32,64]{1,0,2:T(8,128)(2,1)S(1)} %copy.68, f32[256,32]{0,1:T(8,128)S(1)} %sqrt_add_fusion, f32[64]{0:T(128)S(1)} %convert_multiply_fusion.1), kind=kOutput, calls=%fused_computation.12 | convolution fusion | flops 34603008 | bytes 2261248 | tf_op jit(solution)/shard_map/fph,ghf->pfg/dot_general | solution.py:107
  111.3 0.8 copy.69
  112.0 9.6 %add_bitcast_fusion = f32[256,64,32]{0,2,1:T(8,128)S(1)} fusion(f32[64,32,256]{2,1,0:T(8,128)} %fusion.2, bf16[32,32,64]{1,0,2:T(8,128)(2,1)S(1)} %copy.69, f32[256,32]{0,1:T(8,128)S(1)} %sqrt_add_fusion, f32[64]{0:T(128)S(1)} %convert_multiply_fusion.1), kind=kOutput, calls=%fused_computation.9 | convolution fusion | flops 35127296 | bytes 4358400 | tf_op jit(solution)/shard_map/fph,ghf->pfg/dot_general | solution.py:112
  121.6 7.0 %subtract_bitcast_fusion = f32[256,64,32]{0,2,1:T(8,128)S(1)} fusion(f32[64,32,256]{2,1,0:T(8,128)S(1)} %fusion.6, bf16[32,32,64]{1,0,2:T(8,128)(2,1)S(1)} %copy.69, f32[256,32]{0,1:T(8,128)S(1)} %sqrt_add_fusion, f32[64]{0:T(128)S(1)} %convert_multiply_fusion.1), kind=kOutput, calls=%fused_computation.10 | convolution fusion | flops 35127296 | bytes 4358400 | tf_op jit(solution)/shard_map/fph,ghf->pfg/dot_general | solution.py:109
  128.7 2.3 pad_maximum_fusion
  130.9 5.7 %copy.50 = f32[256,4096]{1,0:T(8,128)} copy(f32[256,4096]{0,1:T(8,128)} %bitcast.112) | data formatting | bytes 8388608
  136.6 0.0 reduce-scatter.7.cloned.1.call-update
  136.6 0.0 reduce-scatter.5.cloned.1.call-start
  136.7 54.8 %reduce-scatter.7.cloned.1.call-done = f32[64,4096]{1,0:T(8,128)} async-done(((f32[256,4096]{1,0:T(8,128)}), f32[64,4096]{1,0:T(8,128)}) %reduce-scatter.7.cloned.1.call-update) | async-done | bytes 1048592
  191.5 1.8 copy.51
  193.3 2.7 %copy.47 = f32[64,64,64]{2,1,0:T(8,128)} copy(f32[64,64,64]{0,2,1:T(8,128)S(1)} %bitcast.113) | data formatting | bytes 2097152 | tf_op jit(solution)/shard_map/reduce_scatter | solution.py:28
  196.0 0.0 reduce-scatter.5.cloned.1.call-update
  196.0 47.5 %reduce-scatter.5.cloned.1.call-done = f32[8,64,64]{2,1,0:T(8,128)} async-done(((f32[64,64,64]{2,1,0:T(8,128)}), f32[8,64,64]{2,1,0:T(8,128)}) %reduce-scatter.5.cloned.1.call-update) | async-done | bytes 131088 | tf_op jit(solution)/shard_map/reduce_scatter | solution.py:28
  243.5 1.7 broadcast_multiply_fusion
  (41 shorter events, 0.3 us)
Async XLA Ops:
  6.5 1.0 copy-start
  11.8 18.4 %all-to-all-start = ((bf16[16,64,128]{2,1,0:T(8,128)(2,1)}), bf16[16,64,128]{2,1,0:T(8,128)(2,1)S(1)}, u32[]{:S(2)}, u32[]{:S(2)}) async-start(bf16[16,64,128]{2,1,0:T(8,128)(2,1)} %bitcast.1), calls=%async_computation | async-start | bytes 524288 | tf_op jit(solution)/shard_map/all_to_all | solution.py:79
  19.0 172.5 %reduce-scatter.7.cloned.1.call-start = ((), (), s32[]{:S(2)}) async-start(), calls=%async_computation.4 | async-start | bytes 5242880
  22.3 7.0 %copy-start.1 = (s32[256]{0:T(256)S(1)}, s32[256]{0:T(256)}, u32[]{:S(2)}) copy-start(s32[256]{0:T(256)} %param.7) | copy-start | bytes 3076
  36.2 15.0 %collective-permute-start = (bf16[1,64,128]{2,1,0:T(8,128)(2,1)S(1)}, bf16[1,64,128]{2,1,0:T(8,128)(2,1)S(1)}, u32[]{:S(2)}, u32[]{:S(2)}) collective-permute-start(bf16[1,64,128]{2,1,0:T(8,128)(2,1)S(1)} %bitcast.133), channel_id=1, source_target_pairs={{0,32},{32,0},{64,96},{96,64},{128,160},{160,128},{192,224},{224,1... | collective-permute-start | bytes 49160 | tf_op jit(solution)/shard_map/ppermute | solution.py:92
  39.0 16.4 %collective-permute-start.1 = (bf16[1,64,128]{2,1,0:T(8,128)(2,1)S(1)}, bf16[1,64,128]{2,1,0:T(8,128)(2,1)S(1)}, u32[]{:S(2)}, u32[]{:S(2)}) collective-permute-start(bf16[1,64,128]{2,1,0:T(8,128)(2,1)S(1)} %bitcast.132), channel_id=1, source_target_pairs={{0,64},{32,96},{64,0},{96,32},{128,192},{160,224},{192,128},{224,1... | collective-permute-start | bytes 49160 | tf_op jit(solution)/shard_map/ppermute | solution.py:92
  41.3 16.9 %collective-permute-start.2 = (bf16[1,64,128]{2,1,0:T(8,128)(2,1)S(1)}, bf16[1,64,128]{2,1,0:T(8,128)(2,1)S(1)}, u32[]{:S(2)}, u32[]{:S(2)}) collective-permute-start(bf16[1,64,128]{2,1,0:T(8,128)(2,1)S(1)} %bitcast.131), channel_id=1, source_target_pairs={{0,96},{32,64},{64,32},{96,0},{128,224},{160,192},{192,160},{224,1... | collective-permute-start | bytes 49160 | tf_op jit(solution)/shard_map/ppermute | solution.py:92
  44.2 20.7 %collective-permute-start.3 = (bf16[1,64,128]{2,1,0:T(8,128)(2,1)S(1)}, bf16[1,64,128]{2,1,0:T(8,128)(2,1)S(1)}, u32[]{:S(2)}, u32[]{:S(2)}) collective-permute-start(bf16[1,64,128]{2,1,0:T(8,128)(2,1)S(1)} %bitcast.130), channel_id=1, source_target_pairs={{0,128},{32,160},{64,192},{96,224},{128,0},{160,32},{192,64},{224,... | collective-permute-start | bytes 49160 | tf_op jit(solution)/shard_map/ppermute | solution.py:92
  47.8 20.3 %collective-permute-start.4 = (bf16[1,64,128]{2,1,0:T(8,128)(2,1)S(1)}, bf16[1,64,128]{2,1,0:T(8,128)(2,1)S(1)}, u32[]{:S(2)}, u32[]{:S(2)}) collective-permute-start(bf16[1,64,128]{2,1,0:T(8,128)(2,1)S(1)} %bitcast.129), channel_id=1, source_target_pairs={{0,160},{32,128},{64,224},{96,192},{128,32},{160,0},{192,96},{224,... | collective-permute-start | bytes 49160 | tf_op jit(solution)/shard_map/ppermute | solution.py:92
  51.2 20.5 %collective-permute-start.5 = (bf16[1,64,128]{2,1,0:T(8,128)(2,1)S(1)}, bf16[1,64,128]{2,1,0:T(8,128)(2,1)S(1)}, u32[]{:S(2)}, u32[]{:S(2)}) collective-permute-start(bf16[1,64,128]{2,1,0:T(8,128)(2,1)S(1)} %bitcast.128), channel_id=1, source_target_pairs={{0,192},{32,224},{64,128},{96,160},{128,64},{160,96},{192,0},{224,... | collective-permute-start | bytes 49160 | tf_op jit(solution)/shard_map/ppermute | solution.py:92
  55.4 21.0 %collective-permute-start.6 = (bf16[1,64,128]{2,1,0:T(8,128)(2,1)S(1)}, bf16[1,64,128]{2,1,0:T(8,128)(2,1)S(1)}, u32[]{:S(2)}, u32[]{:S(2)}) collective-permute-start(bf16[1,64,128]{2,1,0:T(8,128)(2,1)S(1)} %bitcast.127), channel_id=1, source_target_pairs={{0,224},{32,192},{64,160},{96,128},{128,96},{160,64},{192,32},{224... | collective-permute-start | bytes 49160 | tf_op jit(solution)/shard_map/ppermute | solution.py:92
  58.2 21.2 %collective-permute-start.7 = (bf16[1,64,128]{2,1,0:T(8,128)(2,1)S(1)}, bf16[1,64,128]{2,1,0:T(8,128)(2,1)S(1)}, u32[]{:S(2)}, u32[]{:S(2)}) collective-permute-start(bf16[1,64,128]{2,1,0:T(8,128)(2,1)S(1)} %bitcast.126), channel_id=1, source_target_pairs={{0,256},{32,288},{64,320},{96,352},{128,384},{160,416},{192,448},{... | collective-permute-start | bytes 49160 | tf_op jit(solution)/shard_map/ppermute | solution.py:92
  64.9 19.6 %collective-permute-start.8 = (bf16[1,64,128]{2,1,0:T(8,128)(2,1)S(1)}, bf16[1,64,128]{2,1,0:T(8,128)(2,1)S(1)}, u32[]{:S(2)}, u32[]{:S(2)}) collective-permute-start(bf16[1,64,128]{2,1,0:T(8,128)(2,1)S(1)} %bitcast.125), channel_id=1, source_target_pairs={{0,288},{32,256},{64,352},{96,320},{128,416},{160,384},{192,480},{... | collective-permute-start | bytes 49160 | tf_op jit(solution)/shard_map/ppermute | solution.py:92
  68.2 19.9 %collective-permute-start.9 = (bf16[1,64,128]{2,1,0:T(8,128)(2,1)S(1)}, bf16[1,64,128]{2,1,0:T(8,128)(2,1)S(1)}, u32[]{:S(2)}, u32[]{:S(2)}) collective-permute-start(bf16[1,64,128]{2,1,0:T(8,128)(2,1)S(1)} %bitcast.124), channel_id=1, source_target_pairs={{0,320},{32,352},{64,256},{96,288},{128,448},{160,480},{192,384},{... | collective-permute-start | bytes 49160 | tf_op jit(solution)/shard_map/ppermute | solution.py:92
  71.7 19.4 %collective-permute-start.10 = (bf16[1,64,128]{2,1,0:T(8,128)(2,1)S(1)}, bf16[1,64,128]{2,1,0:T(8,128)(2,1)S(1)}, u32[]{:S(2)}, u32[]{:S(2)}) collective-permute-start(bf16[1,64,128]{2,1,0:T(8,128)(2,1)S(1)} %bitcast.123), channel_id=1, source_target_pairs={{0,352},{32,320},{64,288},{96,256},{128,480},{160,448},{192,416},{... | collective-permute-start | bytes 49160 | tf_op jit(solution)/shard_map/ppermute | solution.py:92
  76.4 14.8 %collective-permute-start.11 = (bf16[1,64,128]{2,1,0:T(8,128)(2,1)S(1)}, bf16[1,64,128]{2,1,0:T(8,128)(2,1)S(1)}, u32[]{:S(2)}, u32[]{:S(2)}) collective-permute-start(bf16[1,64,128]{2,1,0:T(8,128)(2,1)S(1)} %bitcast.122), channel_id=1, source_target_pairs={{0,384},{32,416},{64,448},{96,480},{128,256},{160,288},{192,320},{... | collective-permute-start | bytes 49160 | tf_op jit(solution)/shard_map/ppermute | solution.py:92
  79.5 11.7 %collective-permute-start.12 = (bf16[1,64,128]{2,1,0:T(8,128)(2,1)S(1)}, bf16[1,64,128]{2,1,0:T(8,128)(2,1)S(1)}, u32[]{:S(2)}, u32[]{:S(2)}) collective-permute-start(bf16[1,64,128]{2,1,0:T(8,128)(2,1)S(1)} %bitcast.121), channel_id=1, source_target_pairs={{0,416},{32,384},{64,480},{96,448},{128,288},{160,256},{192,352},{... | collective-permute-start | bytes 49160 | tf_op jit(solution)/shard_map/ppermute | solution.py:92
  84.5 7.1 %collective-permute-start.13 = (bf16[1,64,128]{2,1,0:T(8,128)(2,1)S(1)}, bf16[1,64,128]{2,1,0:T(8,128)(2,1)S(1)}, u32[]{:S(2)}, u32[]{:S(2)}) collective-permute-start(bf16[1,64,128]{2,1,0:T(8,128)(2,1)S(1)} %bitcast.120), channel_id=1, source_target_pairs={{0,448},{32,480},{64,384},{96,416},{128,320},{160,352},{192,256},{... | collective-permute-start | bytes 49160 | tf_op jit(solution)/shard_map/ppermute | solution.py:92
  88.1 6.3 %collective-permute-start.14 = (bf16[1,64,128]{2,1,0:T(8,128)(2,1)S(1)}, bf16[1,64,128]{2,1,0:T(8,128)(2,1)S(1)}, u32[]{:S(2)}, u32[]{:S(2)}) collective-permute-start(bf16[1,64,128]{2,1,0:T(8,128)(2,1)S(1)} %bitcast.119), channel_id=1, source_target_pairs={{0,480},{32,448},{64,416},{96,384},{128,352},{160,320},{192,288},{... | collective-permute-start | bytes 49160 | tf_op jit(solution)/shard_map/ppermute | solution.py:92
  136.6 106.9 %reduce-scatter.5.cloned.1.call-start = ((), (), s32[]{:S(2)}) async-start(), calls=%async_computation.3 | async-start | bytes 2359296 | tf_op jit(solution)/shard_map/reduce_scatter | solution.py:28
Sparse Core Ops, SparseCore 0:
  136.8 54.6 reduce-scatter.6
  196.2 47.3 reduce-scatter.4
